TPU v7x, 32 devices: a whole 2x2x4 slice. The times are simulated.
32 devices in a mesh: occ: 16 (over z, x, core), vir: 2 (over y).
Axes of the slice: x: 2, y: 2, z: 4, core: 2. Of those that a mesh axis runs over, the one named last changes fastest.
Arguments:
- factors: bfloat16 [16, 1024, 3072], P('occ', 'vir'), may hold values from -0.71875 to 0.71875
- occ_energy: float32 [16], replicated, may hold values from -2 to -0.4
- vir_energy: float32 [1024], replicated, may hold values from 0.4 to 4
- density_in: float32 [16, 1024, 3072], P('occ', 'vir'), may hold values from -3 to 3
Outputs:
- density: float32 [16, 1024, 3072], P('occ', 'vir')
All inputs are finite; a program needn't handle non-finite values.
Results may differ from a plain program's by a relative error of at most 0.0027.
Values may be sent and summed in bfloat16 or wider, within the bound.
A program may use at most 128 MiB of HBM per device.

v0:
```python
import functools

import jax
import jax.numpy as jnp
from jax import lax
from jax.experimental import pallas as pl
from jax.experimental.pallas import tpu as pltpu
from jax.sharding import PartitionSpec as P

MESH = pl.DeviceIdType.MESH
OWN, NEAR, FAR = 0, 1, 2


def product(left, right):
    out = lax.dot_general(
        left, right, (((1,), (1,)), ((), ())), preferred_element_type=jnp.float32
    )
    return out.astype(jnp.bfloat16).astype(jnp.float32)


def kernel(
    n, cycle, e_pair, e_rows, e_cols, factors, density_in, out,
    buf, acc, direct, swapped, send, recv, local,
):
    pairs, _, r, aux = factors.shape
    w = 2 * r
    h = pairs * w
    i, v = lax.axis_index("occ"), lax.axis_index("vir")
    even = lax.rem(i, 2) == 0
    peer = i + 1 - 2 * lax.rem(i, 2)
    ahead, behind = lax.rem(i + 2, cycle), lax.rem(i + cycle - 2, cycle)

    load_own = pltpu.make_async_copy(factors, buf.at[OWN, 0], local.at[0])
    load_acc = pltpu.make_async_copy(density_in, acc, local.at[1])
    load_own.start()
    load_acc.start()

    barrier = pltpu.get_barrier_semaphore()
    for other in (ahead, behind, peer):
        pl.semaphore_signal(barrier, inc=1, device_id={"occ": other}, device_id_type=MESH)
    for d in range(1, n):
        pl.semaphore_signal(barrier, inc=1, device_id={"vir": lax.rem(v + d, n)}, device_id_type=MESH)
    pl.semaphore_wait(barrier, n + 2)

    def move(src, kind, d, p, q, device):
        return pltpu.make_async_remote_copy(
            src_ref=src,
            dst_ref=buf.at[kind, d, p, q],
            send_sem=send.at[kind, d, p, q],
            recv_sem=recv.at[kind, d, p, q],
            device_id=device,
            device_id_type=MESH,
        )

    def arrived(kind, d, p, q):
        move(buf.at[kind, d, p, q], kind, d, p, q, {"occ": peer}).wait_recv()

    def along_vir(d):
        return {"vir": lax.rem(v + d, n)}

    for p in range(pairs):
        for q in range(2):
            for d in range(1, n):
                move(factors.at[p, q], OWN, d, p, q, along_vir(d)).start()
            move(factors.at[p, q], FAR, 0, p, q, {"occ": ahead}).start()

            @pl.when(even)
            def _():
                move(factors.at[p, q], NEAR, 0, p, q, {"occ": peer}).start()

    def block(kind):
        return buf[kind, 0].reshape(h, aux)

    def pair(kind, d, p):
        return buf[kind, d, p].reshape(w, aux)

    tile = 1024 if aux % 1024 == 0 else aux

    def contribute(kind, d, p, m, s):
        denom = e_pair[kind] - e_rows[...] - e_cols[d, p]
        amp = ((2.0 * m - s) / denom).astype(jnp.bfloat16)

        def column(c, _):
            at = pl.ds(pl.multiple_of(c * tile, tile), tile)
            acc[:, at] += jnp.dot(
                amp, buf[kind, d, p, :, :, at].reshape(w, tile), preferred_element_type=jnp.float32
            )
            return 0

        lax.fori_loop(0, aux // tile, column, 0)

    def own_pair(d, p):
        m = product(block(OWN), pair(OWN, d, p))
        contribute(OWN, d, p, m, m)

    load_own.wait()
    load_acc.wait()

    def first(p, _):
        own_pair(0, p)
        return 0

    lax.fori_loop(0, pairs, first, 0)

    def second(p, _):
        for q in range(2):
            arrived(FAR, 0, p, q)

            @pl.when(even == False)
            def _():
                move(buf.at[FAR, 0, p, q], NEAR, 0, p, q, {"occ": peer}).start()

        for d in range(1, n):
            move(buf.at[FAR, 0, p, 0], FAR, d, p, 0, along_vir(d)).start()

        def whole(d, _):
            for q in range(2):
                arrived(OWN, d, p, q)

                @pl.when(even)
                def _():
                    move(buf.at[OWN, d, p, q], NEAR, d, p, q, {"occ": peer}).start()

            move(buf.at[OWN, d, p, 1], FAR, d, p, 1, {"occ": ahead}).start()
            own_pair(d, p)
            return 0

        lax.fori_loop(1, n, whole, 0)
        direct[FAR - 1, p] = product(block(OWN), pair(FAR, 0, p))
        return 0

    lax.fori_loop(0, pairs, second, 0)

    def third(step, _):
        kind = FAR - step

        @pl.when(step == 1)
        def _():
            def near(p, _):
                arrived(NEAR, 0, p, 0)
                arrived(NEAR, 0, p, 1)
                direct[NEAR - 1, p] = product(block(OWN), pair(NEAR, 0, p))
                return 0

            lax.fori_loop(0, pairs, near, 0)

        def diagonal(p, _):
            at = pl.ds(pl.multiple_of(p * w, w), w)
            s = jnp.concatenate([direct[kind - 1, b, at, :].T for b in range(pairs)], axis=0)
            contribute(kind, 0, p, direct[kind - 1, p], s)

            def other(d, _):
                swapped[kind - 1, d, p] = product(block(kind), pair(OWN, d, p))
                return 0

            lax.fori_loop(1, n, other, 0)
            return 0

        lax.fori_loop(0, pairs, diagonal, 0)
        return 0

    lax.fori_loop(0, 2, third, 0)

    def fourth(step, _):
        p, d = step // (n - 1), 1 + lax.rem(step, n - 1)
        for q in range(2):
            arrived(FAR, d, p, q)

            @pl.when(even == False)
            def _():
                move(buf.at[FAR, d, p, q], NEAR, d, p, q, {"occ": peer}).start()

        def finish(turn, _):
            kind = FAR - turn

            @pl.when(turn == 1)
            def _():
                arrived(NEAR, d, p, 0)
                arrived(NEAR, d, p, 1)

            m = product(block(OWN), pair(kind, d, p))
            contribute(kind, d, p, m, swapped[kind - 1, d, p])
            return 0

        lax.fori_loop(0, 2, finish, 0)
        return 0

    lax.fori_loop(0, pairs * (n - 1), fourth, 0)

    store = pltpu.make_async_copy(acc, out, local.at[1])
    store.start()

    for p in range(pairs):
        for q in range(2):
            for kind in (OWN, NEAR, FAR):
                for d in range(1 if kind == OWN else 0, n):
                    move(buf.at[kind, d, p, q], kind, d, p, q, {"occ": peer}).wait_send()
    store.wait()


def on_device(factors, occ_energy, vir_energy, density_in):
    h, aux = factors.shape[1:]
    n, cycle = lax.axis_size("vir"), lax.axis_size("occ")
    i, v = lax.axis_index("occ"), lax.axis_index("vir")
    w = 256 if h % 256 == 0 else h
    pairs = h // w
    e_pair = occ_energy[i] + occ_energy[(i - jnp.arange(3)) % cycle]
    ranks = (v - jnp.arange(n)) % n
    by_rank = vir_energy.reshape(n, h)[ranks]
    vmem = pl.BlockSpec(memory_space=pltpu.VMEM)
    hbm = pl.BlockSpec(memory_space=pl.ANY)
    out = pl.pallas_call(
        functools.partial(kernel, n, cycle),
        out_shape=jax.ShapeDtypeStruct((h, aux), jnp.float32),
        in_specs=[pl.BlockSpec(memory_space=pltpu.SMEM), vmem, vmem, hbm, hbm],
        out_specs=hbm,
        scratch_shapes=[
            pltpu.VMEM((3, n, pairs, 2, w // 2, aux), jnp.bfloat16),
            pltpu.VMEM((h, aux), jnp.float32),
            pltpu.VMEM((2, pairs, h, w), jnp.float32),
            pltpu.VMEM((2, n, pairs, h, w), jnp.float32),
            pltpu.SemaphoreType.DMA((3, n, pairs, 2)),
            pltpu.SemaphoreType.DMA((3, n, pairs, 2)),
            pltpu.SemaphoreType.DMA((2,)),
        ],
        compiler_params=pltpu.CompilerParams(
            collective_id=0, has_side_effects=True, vmem_limit_bytes=60 * 1024 * 1024
        ),
    )(
        e_pair,
        by_rank[0][:, None],
        by_rank.reshape(n, pairs, 1, w),
        factors.reshape(pairs, 2, w // 2, aux),
        density_in.reshape(h, aux),
    )
    return out.reshape(density_in.shape)


def solution(mesh):
    return jax.shard_map(
        on_device,
        mesh=mesh,
        in_specs=(P("occ", "vir", None), P(), P(), P("occ", "vir", None)),
        out_specs=P("occ", "vir", None),
        check_vma=False,
    )
```

profile of v0, /device:TPU:0, one launch (start us, length us, event | category | flops | bytes accessed | tf_op | source)
XLA Modules:
  0.0 130.9 jit_solution(10419168043124761737)
XLA Ops:
  0.0 1.2 dynamic_slice.3
  1.3 1.3 gather_fusion
  2.6 1.2 broadcast_add_fusion.e_pair
  3.8 0.7 reshape.113
  4.5 0.6 gather_fusion.1
  5.0 0.6 reshape.114.e_cols
  5.6 0.9 copy.5.e_rows
  6.5 118.1 %shard_map.46 = f32[512,3072]{1,0:T(8,128)} custom-call(f32[3]{0:T(128)} %broadcast_add_fusion.e_pair, f32[512,1]{1,0:T(8,128)} %copy.5.e_rows, f32[2,2,1,256]{3,2,1,0:T(1,128)} %reshape.114.e_cols, bf16[2,2,128,3072]{3,2,1,0:T(8,128)(2,1)} %bitcast.12, f32[512,3072]{1,0:T(8,128)} %bitcast.11), custom_call_target="tpu_custom_call" | custom-call | tf_op jit(solution)/shard_map/pallas_call | solution.py:212
  124.6 6.2 %copy.7 = f32[1,512,3072]{2,1,0:T(8,128)} copy(f32[1,512,3072]{2,1,0:T(8,128)} %bitcast.10) | data formatting | bytes 12582912
  (5 shorter events, 0.0 us)
where the time goes:
time: 131 us
  Pallas kernels  118 us (90%)
  local copies, waits for them, and re-layouts  11.5 us (9%)
    pallas_call x1, Pallas kernels, on_device(): pl.pallas_call(functools.partial(kernel, n, cycle), out_shape=jax.ShapeDt...  118 us
    unnamed x1, local copies, waits for them, and re-layouts  6.23 us

commit v1 on v0

--- a/solution.py
+++ b/solution.py
@@ -19,8 +19,8 @@
 
 
 def kernel(
-    n, cycle, e_pair, e_rows, e_cols, factors, density_in, out,
-    buf, acc, direct, swapped, send, recv, local,
+    n, cycle, e_occ, e_vir, factors, density_in, out,
+    buf, acc, direct, swapped, e_rows, send, recv, local,
 ):
     pairs, _, r, aux = factors.shape
     w = 2 * r
@@ -76,8 +76,13 @@
 
     tile = 1024 if aux % 1024 == 0 else aux
 
-    def contribute(kind, d, p, m, s):
-        denom = e_pair[kind] - e_rows[...] - e_cols[d, p]
+    def store(c):
+        at = pl.ds(pl.multiple_of(c * tile, tile), tile)
+        return pltpu.make_async_copy(acc.at[:, at], out.at[:, at], local.at[2 + c])
+
+    def contribute(kind, d, p, m, s, last=None):
+        partner = e_occ[lax.rem(i - kind + cycle, cycle)]
+        denom = e_occ[i] + partner - e_rows[:, :1] - e_vir[lax.rem(v - d + n, n), p]
         amp = ((2.0 * m - s) / denom).astype(jnp.bfloat16)
 
         def column(c, _):
@@ -85,6 +90,12 @@
             acc[:, at] += jnp.dot(
                 amp, buf[kind, d, p, :, :, at].reshape(w, tile), preferred_element_type=jnp.float32
             )
+            if last is not None:
+
+                @pl.when(last)
+                def _():
+                    store(c).start()
+
             return 0
 
         lax.fori_loop(0, aux // tile, column, 0)
@@ -93,6 +104,8 @@
         m = product(block(OWN), pair(OWN, d, p))
         contribute(OWN, d, p, m, m)
 
+    for p in range(pairs):
+        e_rows[p * w : (p + 1) * w, :] = jnp.broadcast_to(e_vir[v, p], (128, w)).T
     load_own.wait()
     load_acc.wait()
 
@@ -179,57 +192,52 @@
                 arrived(NEAR, d, p, 1)
 
             m = product(block(OWN), pair(kind, d, p))
-            contribute(kind, d, p, m, swapped[kind - 1, d, p])
+            last = (step == pairs * (n - 1) - 1) & (turn == 1)
+            contribute(kind, d, p, m, swapped[kind - 1, d, p], last)
             return 0
 
         lax.fori_loop(0, 2, finish, 0)
         return 0
 
     lax.fori_loop(0, pairs * (n - 1), fourth, 0)
-
-    store = pltpu.make_async_copy(acc, out, local.at[1])
-    store.start()
 
     for p in range(pairs):
         for q in range(2):
             for kind in (OWN, NEAR, FAR):
                 for d in range(1 if kind == OWN else 0, n):
                     move(buf.at[kind, d, p, q], kind, d, p, q, {"occ": peer}).wait_send()
-    store.wait()
+    for c in range(aux // tile):
+        store(c).wait()
 
 
 def on_device(factors, occ_energy, vir_energy, density_in):
     h, aux = factors.shape[1:]
     n, cycle = lax.axis_size("vir"), lax.axis_size("occ")
-    i, v = lax.axis_index("occ"), lax.axis_index("vir")
     w = 256 if h % 256 == 0 else h
     pairs = h // w
-    e_pair = occ_energy[i] + occ_energy[(i - jnp.arange(3)) % cycle]
-    ranks = (v - jnp.arange(n)) % n
-    by_rank = vir_energy.reshape(n, h)[ranks]
     vmem = pl.BlockSpec(memory_space=pltpu.VMEM)
     hbm = pl.BlockSpec(memory_space=pl.ANY)
     out = pl.pallas_call(
         functools.partial(kernel, n, cycle),
         out_shape=jax.ShapeDtypeStruct((h, aux), jnp.float32),
-        in_specs=[pl.BlockSpec(memory_space=pltpu.SMEM), vmem, vmem, hbm, hbm],
+        in_specs=[pl.BlockSpec(memory_space=pltpu.SMEM), vmem, hbm, hbm],
         out_specs=hbm,
         scratch_shapes=[
             pltpu.VMEM((3, n, pairs, 2, w // 2, aux), jnp.bfloat16),
             pltpu.VMEM((h, aux), jnp.float32),
             pltpu.VMEM((2, pairs, h, w), jnp.float32),
             pltpu.VMEM((2, n, pairs, h, w), jnp.float32),
+            pltpu.VMEM((h, 128), jnp.float32),
             pltpu.SemaphoreType.DMA((3, n, pairs, 2)),
             pltpu.SemaphoreType.DMA((3, n, pairs, 2)),
-            pltpu.SemaphoreType.DMA((2,)),
+            pltpu.SemaphoreType.DMA((2 + max(1, aux // 1024),)),
         ],
         compiler_params=pltpu.CompilerParams(
             collective_id=0, has_side_effects=True, vmem_limit_bytes=60 * 1024 * 1024
         ),
     )(
-        e_pair,
-        by_rank[0][:, None],
-        by_rank.reshape(n, pairs, 1, w),
+        occ_energy,
+        vir_energy.reshape(n, pairs, 1, w),
         factors.reshape(pairs, 2, w // 2, aux),
         density_in.reshape(h, aux),
     )

time: 131 us -> 123 us (0.939)
  local copies, waits for them, and re-layouts: 11.5 us -> 6.23 us
    gather x2 -> x0, local copies, waits for them, and re-layouts: 1.85 us -> none  [the longest x1 1.3 us: on_device(): e_pair = occ_energy[i] + occ_energy[(i - jnp.arange(3)) % cycle]]
where the time goes in v1:
time: 123 us
  Pallas kernels  117 us (95%)
  local copies, waits for them, and re-layouts  6.23 us (5%)
    pallas_call x1, Pallas kernels, on_device(): pl.pallas_call(functools.partial(kernel, n, cycle), out_shape=jax.ShapeDt...  117 us
    unnamed x1, local copies, waits for them, and re-layouts  6.23 us

profile of v1, /device:TPU:0, one launch (start us, length us, event | category | flops | bytes accessed | tf_op | source)
XLA Modules:
  0.0 123.1 jit_solution(2460692237590692640)
XLA Ops:
  0.0 116.9 %shard_map.46 = f32[512,3072]{1,0:T(8,128)} custom-call(f32[16]{0:T(128)} %e_occ.1, f32[2,2,1,256]{3,2,1,0:T(1,128)} %bitcast.7, bf16[2,2,128,3072]{3,2,1,0:T(8,128)(2,1)} %bitcast.6, f32[512,3072]{1,0:T(8,128)} %bitcast.5), custom_call_target="tpu_custom_call" | custom-call | tf_op jit(solution)/shard_map/pallas_call | solution.py:220
  116.9 6.2 %copy.6 = f32[1,512,3072]{2,1,0:T(8,128)} copy(f32[1,512,3072]{2,1,0:T(8,128)} %bitcast.4) | data formatting | bytes 12582912
